TPU v7x, 256 devices: a whole 4x4x8 slice. The times are simulated.
256 devices in a mesh: row: 4 (over x), col: 64 (over y, z, core).
Axes of the slice: x: 4, y: 4, z: 8, core: 2. Of those that a mesh axis runs over, the one named last changes fastest.
Arguments:
- activations: bfloat16 [8, 256, 8192], P('row')
- out_grads: bfloat16 [8, 256, 28672], P('row', None, 'col')
- valid_len: int32 [8], P('row'), may hold values from 1 to 256, 1024 in all
- weight: bfloat16 [8192, 28672], P('row', 'col'), may hold values from -0.0625 to 0.0625
- sketch: bfloat16 [28672, 512], P('col'), may hold values from -6 to 6
Outputs:
- basis: float32 [8192, 512], P(('row', 'col'))
- coeffs: float32 [512, 28672], P('row', 'col')
Inputs may be any that keep to these rules, and one draw needn't show every extreme that they name: `valid_len`: valid tokens of each sequence; at least one sequence fills all 256 slots.
All inputs are finite; a program needn't handle non-finite values. No bound on the sum of `valid_len` on one device may be relied on, other than what follows from the above.
Results may differ from a plain program's by a relative error of at most 0.01.
Values may be sent and summed in bfloat16 or wider, within the bound.
A program may use at most 64 MiB of HBM per device.

v0:
```python
import math
import jax
import jax.numpy as jnp
from jax import lax
from jax.sharding import PartitionSpec as P


def contract_rows(left, right):
    return lax.dot_general(
        left, right, (((0,), (0,)), ((), ())), preferred_element_type=jnp.float32
    )


def gram_local(sketch_rows):
    return lax.dot_general(
        sketch_rows, sketch_rows, (((0,), (0,)), ((), ())), precision=lax.Precision.HIGHEST
    )


def solve_basis(gram, sketch_rows):
    factor_low = jnp.linalg.cholesky(gram)
    return lax.linalg.triangular_solve(
        factor_low, sketch_rows, left_side=False, lower=True, transpose_a=True
    )


def orthonormal_shared(sketch_rows):
    gram = lax.psum(gram_local(sketch_rows), ("row", "col"))
    return solve_basis(gram, sketch_rows)


def reduce_sketch(left, right):
    return lax.psum_scatter(
        jnp.dot(left, right, preferred_element_type=jnp.float32),
        "col",
        scatter_dimension=0,
        tiled=True,
    )


def local(activations, out_grads, valid_len, weight, sketch):
    seq_dev, length, model_width = activations.shape
    rows_here, cols_here = weight.shape
    col_count = lax.axis_size("col")
    col_index = lax.axis_index("col")
    row_index = lax.axis_index("row")
    own_rows = rows_here // col_count
    own_start = col_index * own_rows
    positions = lax.iota(jnp.int32, length)
    raw_sketch = reduce_sketch(weight, sketch)
    partial_mass = jnp.zeros((model_width,), jnp.float32)
    for seq_index in range(seq_dev):
        valid = (positions < valid_len[seq_index]).astype(jnp.bfloat16)
        grad_block = contract_rows(activations[seq_index], out_grads[seq_index] * valid[:, None])
        partial_mass = partial_mass + jnp.sum(grad_block * grad_block, axis=1)
    fisher = lax.psum(partial_mass, ("row", "col"))
    total_mass = jnp.sum(fisher)
    own_mass = lax.dynamic_slice_in_dim(fisher, row_index * rows_here, rows_here, 0)
    row_scale = jnp.sqrt(own_mass / (total_mass / model_width + 1e-06))
    first_sketch = (
        lax.dynamic_slice_in_dim(row_scale, own_start, own_rows, 0)[:, None] * raw_sketch
    ).astype(jnp.bfloat16)
    scaled = (row_scale[:, None] * weight.astype(jnp.float32)).astype(jnp.bfloat16)
    proj_part = contract_rows(scaled, lax.all_gather(first_sketch, "col", axis=0, tiled=True))
    projected = lax.psum(proj_part, "row").astype(jnp.bfloat16)
    second_sketch = reduce_sketch(scaled, projected)
    second_basis = orthonormal_shared(second_sketch)
    group_second = lax.all_gather(second_basis.astype(jnp.bfloat16), "col", axis=0, tiled=True)
    coeff_raw = lax.psum_scatter(
        contract_rows(group_second, scaled).astype(jnp.bfloat16),
        "row",
        scatter_dimension=0,
        tiled=True,
    ).astype(jnp.float32)
    return (second_basis * math.sqrt(model_width), coeff_raw * math.sqrt(cols_here * col_count))


def solution(mesh):
    placed = (
        P("row", None, None),
        P("row", None, "col"),
        P("row"),
        P("row", "col"),
        P("col", None),
    )
    return jax.shard_map(
        local,
        mesh=mesh,
        in_specs=placed,
        out_specs=(P(("row", "col"), None), P("row", "col")),
        check_vma=False,
    )
```

profile of v0, /device:TPU:8, one launch (start us, length us, event | category | flops | bytes accessed | tf_op | source)
XLA Modules:
  0.0 952.2 jit_solution(8031663152801272860)
XLA Ops:
  8.2 4.7 fusion.51
  15.5 4.3 multiply_reduce_fusion
  19.8 4.4 multiply_reduce_fusion.1
  24.2 78.7 %psum.21 = f32[8192]{0:T(1024)S(1)} all-reduce(f32[8192]{0:T(1024)S(1)} %add.64), channel_id=1, replica_groups=mesh['row'=4,'col'=64] {'row','col'}, use_global_device_ids=true, to_apply=%region_2.0 | all-reduce | flops 8192 | bytes 65536 | tf_op jit(solution)/shard_map/psum | solution.py:56
  104.3 55.4 %reduce-scatter.6.cloned.1.call-done = f32[32,512]{1,0:T(8,128)} async-done(((f32[2048,512]{1,0:T(8,128)}), f32[32,512]{1,0:T(8,128)}) %reduce-scatter.6.cloned.1.call-update) | async-done | bytes 65552 | tf_op jit(solution)/shard_map/reduce_scatter | solution.py:33
  159.7 1.5 multiply_convert_fusion.6
  161.3 77.5 %all-gather.3.cloned.1.call-done = bf16[2048,512]{1,0:T(8,128)(2,1)} async-done(((bf16[32,512]{1,0:T(8,128)(2,1)}), bf16[2048,512]{1,0:T(8,128)(2,1)}) %all-gather.3.cloned.1.call-update) | async-done | bytes 2097168 | tf_op jit(solution)/shard_map/all_gather | solution.py:64
  238.8 3.6 fusion.6
  242.5 27.8 %all-reduce.5 = bf16[448,512]{1,0:T(8,128)(2,1)S(1)} all-reduce(f32[448,512]{1,0:T(8,128)} %fusion.6), channel_id=1, replica_groups=mesh['row'=4,'col'=64] {'row'}, use_global_device_ids=true, to_apply=%region_5.0 | all-reduce | flops 229376 | bytes 1376256 | tf_op jit(solution)/shard_map/psum | solution.py:65
  270.2 3.2 fusion.5
  273.5 141.3 %reduce-scatter.8.cloned.1.call-done = f32[32,512]{1,0:T(8,128)} async-done(((f32[2048,512]{1,0:T(8,128)}), f32[32,512]{1,0:T(8,128)}) %reduce-scatter.8.cloned.1.call-update) | async-done | bytes 65552 | tf_op jit(solution)/shard_map/reduce_scatter | solution.py:33
  414.8 3.0 fusion.52
  418.8 259.1 %all-reduce.4.cloned.1.call-done = f32[512,512]{0,1:T(8,128)} async-done(((f32[512,512]{0,1:T(8,128)}), f32[512,512]{0,1:T(8,128)}) %all-reduce.4.cloned.1.call-update) | async-done | bytes 1048592 | tf_op jit(solution)/shard_map/psum | solution.py:28
  677.9 1.6 copy.10
  682.0 11.7 %cholesky.104 = f32[128,128]{1,0:T(8,128)S(1)} custom-call(f32[128,128]{1,0:T(8,128)S(1)} %cholesky.266), custom_call_target="Cholesky" | custom-call | tf_op jit(solution)/shard_map/jit(cholesky)/cholesky | solution.py:21
  693.8 9.8 %custom-call.30 = f32[1,128,128]{1,2,0:T(8,128)S(1)} custom-call(f32[1,128,128]{2,1,0:T(8,128)S(1)} %get-tuple-element.29), custom_call_target="InvertDiagBlocksLowerTriangular" | custom-call | tf_op jit(solution)/shard_map/jit(cholesky)/cholesky | solution.py:21
  706.8 13.2 %cholesky.217 = f32[128,128]{1,0:T(8,128)} custom-call(f32[128,128]{1,0:T(8,128)} %cholesky.270), custom_call_target="Cholesky" | custom-call | tf_op jit(solution)/shard_map/jit(cholesky)/cholesky | solution.py:21
  720.0 1.5 select_reduce_fusion.2
  721.5 11.4 %custom-call.31 = f32[1,128,128]{1,2,0:T(8,128)} custom-call(f32[1,128,128]{2,1,0:T(8,128)} %get-tuple-element.26), custom_call_target="InvertDiagBlocksLowerTriangular" | custom-call | tf_op jit(solution)/shard_map/jit(cholesky)/cholesky | solution.py:21
  735.9 13.2 %cholesky.238 = f32[128,128]{1,0:T(8,128)} custom-call(f32[128,128]{1,0:T(8,128)} %cholesky.275), custom_call_target="Cholesky" | custom-call | tf_op jit(solution)/shard_map/jit(cholesky)/cholesky | solution.py:21
  749.1 1.5 select_reduce_fusion.1
  751.3 11.3 %custom-call.32 = f32[1,128,128]{1,2,0:T(8,128)} custom-call(f32[1,128,128]{2,1,0:T(8,128)} %get-tuple-element.23), custom_call_target="InvertDiagBlocksLowerTriangular" | custom-call | tf_op jit(solution)/shard_map/jit(cholesky)/cholesky | solution.py:21
  764.9 11.7 %cholesky.255 = f32[128,128]{1,0:T(8,128)S(1)} custom-call(f32[128,128]{1,0:T(8,128)S(1)} %convolution_subtract_fusion.2), custom_call_target="Cholesky" | custom-call | tf_op jit(solution)/shard_map/jit(cholesky)/cholesky | solution.py:21
  782.4 14.0 %while.1 = (s32[]{:T(128)}, f32[512,512]{1,0:T(8,128)}, s32[4,2]{0,1:T(2,128)S(1)}, f32[4,128,128]{2,1,0:T(8,128)}, s32[]{:T(128)}) while((s32[]{:T(128)}, f32[512,512]{1,0:T(8,128)}, s32[4,2]{0,1:T(2,128)S(1)}, f32[4,128,128]{2,1,0:T(8,128)}, s32[]{:T(128)}) %tuple.32), condition=%wide.while_cond, body=%wide.while_body.sunk | while | flops 2 | bytes 132705 | solution.py:22
  783.0 2.9 bitcast_dynamic-update-slice_fusion.2
  786.5 2.9 bitcast_dynamic-update-slice_fusion.2
  790.0 2.9 bitcast_dynamic-update-slice_fusion.2
  793.5 2.8 bitcast_dynamic-update-slice_fusion.2
  796.3 40.1 %custom-call.33 = f32[4,128,128]{1,2,0:T(8,128)S(1)} custom-call(f32[4,128,128]{2,1,0:T(8,128)} %get-tuple-element.9), custom_call_target="InvertDiagBlocksLowerTriangular" | custom-call | tf_op jit(solution)/shard_map/triangular_solve | solution.py:22
  841.4 75.5 %all-gather.5.cloned.1.call-done = bf16[2048,512]{1,0:T(8,128)(2,1)} async-done(((bf16[32,512]{1,0:T(8,128)(2,1)}), bf16[2048,512]{1,0:T(8,128)(2,1)}) %all-gather.5.cloned.1.call-update) | async-done | bytes 2097168 | tf_op jit(solution)/shard_map/all_gather | solution.py:68
  916.8 2.7 fusion.7
  921.2 22.2 %reduce-scatter.10.cloned.1.call-done = bf16[128,448]{1,0:T(8,128)(2,1)} async-done(((bf16[512,448]{1,0:T(8,128)(2,1)}), bf16[128,448]{1,0:T(8,128)(2,1)}) %reduce-scatter.10.cloned.1.call-update) | async-done | bytes 114704
  (71 shorter events, 30.9 us)
Async XLA Ops:
  7.2 1.0 copy-start
  7.2 152.5 %reduce-scatter.6.cloned.1.call-start = ((), (), s32[]{:S(2)}) async-start(), calls=%async_computation.3 | async-start | bytes 4259840 | tf_op jit(solution)/shard_map/reduce_scatter | solution.py:33
  12.9 0.7 copy-start.4
  12.9 2.6 copy-start.5
  12.9 225.9 %all-gather.3.cloned.1.call-start = ((), (), s32[]{:S(2)}) async-start(), calls=%async_computation.4 | async-start | bytes 2129920 | tf_op jit(solution)/shard_map/all_gather | solution.py:64
  19.8 219.0 %copy-start.1 = (bf16[2048,448]{0,1:T(8,128)(2,1)S(1)}, bf16[2048,448]{0,1:T(8,128)(2,1)}, u32[]{:S(2)}) copy-start(bf16[2048,448]{0,1:T(8,128)(2,1)} %param.8) | copy-start | bytes 5505028
  161.3 253.6 %reduce-scatter.8.cloned.1.call-start = ((), (), s32[]{:S(2)}) async-start(), calls=%async_computation.5 | async-start | bytes 4259840 | tf_op jit(solution)/shard_map/reduce_scatter | solution.py:33
  273.5 404.4 %all-reduce.4.cloned.1.call-start = ((), (), s32[]{:S(2)}) async-start(), calls=%async_computation.6 | async-start | bytes 2097152 | tf_op jit(solution)/shard_map/psum | solution.py:28
  417.8 499.0 %all-gather.5.cloned.1.call-start = ((), (), s32[]{:S(2)}) async-start(), calls=%async_computation.7 | async-start | bytes 2129920 | tf_op jit(solution)/shard_map/all_gather | solution.py:68
  680.9 1.0 copy-start.2
  734.0 102.5 %copy-start.3 = (f32[32,512]{1,0:T(8,128)S(1)}, f32[32,512]{1,0:T(8,128)}, u32[]{:S(2)}) copy-start(f32[32,512]{1,0:T(8,128)} %reduce-scatter.8.cloned.1.call-done) | copy-start | bytes 196612
  841.3 102.1 %reduce-scatter.10.cloned.1.call-start = ((), (), s32[]{:S(2)}) async-start(), calls=%async_computation.8 | async-start | bytes 655360
Sparse Core Ops, SparseCore 0:
  13.1 146.6 reduce-scatter.5
  163.1 75.7 all-gather.2
  273.6 141.1 reduce-scatter.7
  420.1 257.7 all-reduce.3
  841.4 75.3 all-gather.4
  920.7 22.6 reduce-scatter.9
where the time goes:
time: 961 us; the launch traced here: 952 us
  waiting for transfers between devices  631 us (66%)
  other arithmetic  136 us (14%)
  blocking collectives  106 us (11%)
  matrix products  37.2 us (4%)
  local copies, waits for them, and re-layouts  22.7 us (2%)
  between operations  17.8 us (2%)
    psum x1, waiting for transfers between devices, orthonormal_shared(): gram = lax.psum(gram_local(sketch_rows), ('row', 'col'))  259 us
    reduce_scatter x2, waiting for transfers between devices, reduce_sketch(): lax.psum_scatter(jnp.dot(left, right, preferred_element_type=jnp.float32)...  197 us
    another operation x14, other arithmetic, solve_basis(): factor_low = jnp.linalg.cholesky(gram)  87.3 us
    psum x1, blocking collectives, local(): fisher = lax.psum(partial_mass, ('row', 'col'))  78.7 us
    all_gather x1, waiting for transfers between devices, local(): lax.all_gather(first_sketch, 'col', axis=0, tiled=True)  77.5 us
    all_gather x1, waiting for transfers between devices, local(): lax.all_gather(second_basis.astype(jnp.bfloat16), 'col', axis=0, tiled=True)  75.5 us
    another operation x3, other arithmetic, solve_basis(): lax.linalg.triangular_solve(factor_low, sketch_rows, left_side=False, low...  42 us
    psum x1, blocking collectives, local(): projected = lax.psum(proj_part, 'row').astype(jnp.bfloat16)  27.8 us
  transfers between devices with their start and end apart: 6, of which 6 were waited for; matrix products, arithmetic and copies ran while one was open for 1% of the time, Pallas kernels for 0%

commit v1 on v0

--- a/solution.py
+++ b/solution.py
@@ -53,7 +53,7 @@
         valid = (positions < valid_len[seq_index]).astype(jnp.bfloat16)
         grad_block = contract_rows(activations[seq_index], out_grads[seq_index] * valid[:, None])
         partial_mass = partial_mass + jnp.sum(grad_block * grad_block, axis=1)
-    fisher = lax.psum(partial_mass, ("row", "col"))
+    fisher = jnp.sum(lax.all_gather(partial_mass, ("row", "col")), axis=0)
     total_mass = jnp.sum(fisher)
     own_mass = lax.dynamic_slice_in_dim(fisher, row_index * rows_here, rows_here, 0)
     row_scale = jnp.sqrt(own_mass / (total_mass / model_width + 1e-06))

time: 961 us -> 971 us (1.010)
  blocking collectives: 106 us -> 27.7 us
  waiting for transfers between devices: 631 us -> 703 us
    all_gather x0 -> x1, waiting for transfers between devices: none -> 118 us  [local(): fisher = jnp.sum(lax.all_gather(partial_mass, ('row', 'col')), axis=0)]
    psum x1 -> x0, blocking collectives: 78.7 us -> none  [local(): fisher = lax.psum(partial_mass, ('row', 'col'))]
    reduce_scatter x2, waiting for transfers between devices: 197 us -> 153 us  [reduce_sketch(): lax.psum_scatter(jnp.dot(left, right, preferred_element_type=jnp.float32)...]
    unnamed x7 -> x8, waiting for transfers between devices: 22.3 us -> 22.5 us
  transfers between devices with their start and end apart: 6 -> 7, of which waited for: 6 -> 7; matrix products, arithmetic and copies ran while one was open for 1% -> 2% of each run, Pallas kernels for 0% -> 0%
where the time goes in v1:
time: 971 us; the launch traced here: 962 us
  waiting for transfers between devices  703 us (72%)
  other arithmetic  145 us (15%)
  matrix products  33.6 us (3%)
  local copies, waits for them, and re-layouts  31.5 us (3%)
  blocking collectives  27.7 us (3%)
  between operations  19.2 us (2%)
    psum x1, waiting for transfers between devices, orthonormal_shared(): gram = lax.psum(gram_local(sketch_rows), ('row', 'col'))  257 us
    reduce_scatter x2, waiting for transfers between devices, reduce_sketch(): lax.psum_scatter(jnp.dot(left, right, preferred_element_type=jnp.float32)...  153 us
    all_gather x1, waiting for transfers between devices, local(): fisher = jnp.sum(lax.all_gather(partial_mass, ('row', 'col')), axis=0)  118 us
    another operation x14, other arithmetic, solve_basis(): factor_low = jnp.linalg.cholesky(gram)  87.3 us
    all_gather x1, waiting for transfers between devices, local(): lax.all_gather(first_sketch, 'col', axis=0, tiled=True)  77.3 us
    all_gather x1, waiting for transfers between devices, local(): lax.all_gather(second_basis.astype(jnp.bfloat16), 'col', axis=0, tiled=True)  75.3 us
    another operation x3, other arithmetic, solve_basis(): lax.linalg.triangular_solve(factor_low, sketch_rows, left_side=False, low...  42 us
    psum x1, blocking collectives, local(): projected = lax.psum(proj_part, 'row').astype(jnp.bfloat16)  27.7 us
  transfers between devices with their start and end apart: 7, of which 7 were waited for; matrix products, arithmetic and copies ran while one was open for 2% of the time, Pallas kernels for 0%

profile of v1, /device:TPU:8, one launch (start us, length us, event | category | flops | bytes accessed | tf_op | source)
XLA Modules:
  0.0 961.5 jit_solution(7915771263687063306)
XLA Ops:
  10.7 4.5 multiply_reduce_fusion.1
  15.5 2.1 multiply_reduce_fusion
  18.3 3.2 fusion.51
  21.6 118.0 %all-gather.9.cloned.1.call-done = f32[2097152]{0:T(1024)} async-done(((f32[8192]{0:T(1024)}), f32[2097152]{0:T(1024)}) %all-gather.9.cloned.1.call-update) | async-done | bytes 8388624 | tf_op jit(solution)/shard_map/all_gather | solution.py:56
  139.6 9.4 reshape.98
  149.0 3.8 reduce_sum.38
  152.8 5.2 reduce_sum.39
  158.7 12.0 %reduce-scatter.6.cloned.1.call-done = f32[32,512]{1,0:T(8,128)} async-done(((f32[2048,512]{1,0:T(8,128)}), f32[32,512]{1,0:T(8,128)}) %reduce-scatter.6.cloned.1.call-update) | async-done | bytes 65552 | tf_op jit(solution)/shard_map/reduce_scatter | solution.py:33
  172.4 77.3 %all-gather.5.cloned.1.call-done = bf16[2048,512]{1,0:T(8,128)(2,1)} async-done(((bf16[32,512]{1,0:T(8,128)(2,1)}), bf16[2048,512]{1,0:T(8,128)(2,1)}) %all-gather.5.cloned.1.call-update) | async-done | bytes 2097168 | tf_op jit(solution)/shard_map/all_gather | solution.py:64
  249.7 3.6 fusion.6
  253.3 27.7 %all-reduce.5 = bf16[448,512]{1,0:T(8,128)(2,1)S(1)} all-reduce(f32[448,512]{1,0:T(8,128)} %fusion.6), channel_id=1, replica_groups=mesh['row'=4,'col'=64] {'row'}, use_global_device_ids=true, to_apply=%region_5.0 | all-reduce | flops 229376 | bytes 1376256 | tf_op jit(solution)/shard_map/psum | solution.py:65
  281.1 3.2 fusion.5
  284.4 141.1 %reduce-scatter.8.cloned.1.call-done = f32[32,512]{1,0:T(8,128)} async-done(((f32[2048,512]{1,0:T(8,128)}), f32[32,512]{1,0:T(8,128)}) %reduce-scatter.8.cloned.1.call-update) | async-done | bytes 65552 | tf_op jit(solution)/shard_map/reduce_scatter | solution.py:33
  425.5 3.0 fusion.52
  429.5 257.2 %all-reduce.4.cloned.1.call-done = f32[512,512]{0,1:T(8,128)} async-done(((f32[512,512]{0,1:T(8,128)}), f32[512,512]{0,1:T(8,128)}) %all-reduce.4.cloned.1.call-update) | async-done | bytes 1048592 | tf_op jit(solution)/shard_map/psum | solution.py:28
  686.7 1.6 copy.12
  690.7 11.7 %cholesky.104 = f32[128,128]{1,0:T(8,128)S(1)} custom-call(f32[128,128]{1,0:T(8,128)S(1)} %cholesky.266), custom_call_target="Cholesky" | custom-call | tf_op jit(solution)/shard_map/jit(cholesky)/cholesky | solution.py:21
  702.6 9.8 %custom-call.30 = f32[1,128,128]{1,2,0:T(8,128)S(1)} custom-call(f32[1,128,128]{2,1,0:T(8,128)S(1)} %get-tuple-element.29), custom_call_target="InvertDiagBlocksLowerTriangular" | custom-call | tf_op jit(solution)/shard_map/jit(cholesky)/cholesky | solution.py:21
  715.6 13.2 %cholesky.217 = f32[128,128]{1,0:T(8,128)} custom-call(f32[128,128]{1,0:T(8,128)} %cholesky.270), custom_call_target="Cholesky" | custom-call | tf_op jit(solution)/shard_map/jit(cholesky)/cholesky | solution.py:21
  730.2 11.4 %custom-call.31 = f32[1,128,128]{1,2,0:T(8,128)} custom-call(f32[1,128,128]{2,1,0:T(8,128)} %get-tuple-element.26), custom_call_target="InvertDiagBlocksLowerTriangular" | custom-call | tf_op jit(solution)/shard_map/jit(cholesky)/cholesky | solution.py:21
  744.7 13.2 %cholesky.238 = f32[128,128]{1,0:T(8,128)} custom-call(f32[128,128]{1,0:T(8,128)} %cholesky.275), custom_call_target="Cholesky" | custom-call | tf_op jit(solution)/shard_map/jit(cholesky)/cholesky | solution.py:21
  760.1 11.3 %custom-call.32 = f32[1,128,128]{1,2,0:T(8,128)} custom-call(f32[1,128,128]{2,1,0:T(8,128)} %get-tuple-element.23), custom_call_target="InvertDiagBlocksLowerTriangular" | custom-call | tf_op jit(solution)/shard_map/jit(cholesky)/cholesky | solution.py:21
  773.7 11.7 %cholesky.255 = f32[128,128]{1,0:T(8,128)S(1)} custom-call(f32[128,128]{1,0:T(8,128)S(1)} %convolution_subtract_fusion.2), custom_call_target="Cholesky" | custom-call | tf_op jit(solution)/shard_map/jit(cholesky)/cholesky | solution.py:21
  791.2 14.0 %while.1 = (s32[]{:T(128)}, f32[512,512]{1,0:T(8,128)}, s32[4,2]{0,1:T(2,128)S(1)}, f32[4,128,128]{2,1,0:T(8,128)}, s32[]{:T(128)}) while((s32[]{:T(128)}, f32[512,512]{1,0:T(8,128)}, s32[4,2]{0,1:T(2,128)S(1)}, f32[4,128,128]{2,1,0:T(8,128)}, s32[]{:T(128)}) %tuple.32), condition=%wide.while_cond, body=%wide.while_body.sunk | while | flops 2 | bytes 132205 | solution.py:22
  791.8 2.9 bitcast_dynamic-update-slice_fusion.2
  795.3 2.9 bitcast_dynamic-update-slice_fusion.2
  798.8 2.9 bitcast_dynamic-update-slice_fusion.2
  802.3 2.8 bitcast_dynamic-update-slice_fusion.2
  805.1 40.1 %custom-call.33 = f32[4,128,128]{1,2,0:T(8,128)S(1)} custom-call(f32[4,128,128]{2,1,0:T(8,128)} %get-tuple-element.9), custom_call_target="InvertDiagBlocksLowerTriangular" | custom-call | tf_op jit(solution)/shard_map/triangular_solve | solution.py:22
  850.1 75.3 %all-gather.7.cloned.1.call-done = bf16[2048,512]{1,0:T(8,128)(2,1)} async-done(((bf16[32,512]{1,0:T(8,128)(2,1)}), bf16[2048,512]{1,0:T(8,128)(2,1)}) %all-gather.7.cloned.1.call-update) | async-done | bytes 2097168 | tf_op jit(solution)/shard_map/all_gather | solution.py:68
  925.5 2.7 fusion.7
  929.8 22.3 %reduce-scatter.10.cloned.1.call-done = bf16[128,448]{1,0:T(8,128)(2,1)} async-done(((bf16[512,448]{1,0:T(8,128)(2,1)}), bf16[128,448]{1,0:T(8,128)(2,1)}) %reduce-scatter.10.cloned.1.call-update) | async-done | bytes 114704
  (75 shorter events, 34.9 us)
Async XLA Ops:
  8.0 10.3 %copy-start = (bf16[448,512]{1,0:T(8,128)(2,1)S(1)}, bf16[448,512]{1,0:T(8,128)(2,1)}, u32[]{:S(2)}) copy-start(bf16[448,512]{1,0:T(8,128)(2,1)} %param.9) | copy-start | bytes 1376260
  8.0 131.6 %all-gather.9.cloned.1.call-start = ((), (), s32[]{:S(2)}) async-start(), calls=%async_computation.8 | async-start | bytes 8421376 | tf_op jit(solution)/shard_map/all_gather | solution.py:56
  10.7 4.8 copy-start.4
  10.7 4.8 copy-start.5
  15.5 2.8 copy-start.1
  18.2 152.5 %reduce-scatter.6.cloned.1.call-start = ((), (), s32[]{:S(2)}) async-start(), calls=%async_computation.3 | async-start | bytes 4259840 | tf_op jit(solution)/shard_map/reduce_scatter | solution.py:33
  21.5 228.2 %all-gather.5.cloned.1.call-start = ((), (), s32[]{:S(2)}) async-start(), calls=%async_computation.4 | async-start | bytes 2129920 | tf_op jit(solution)/shard_map/all_gather | solution.py:64
  172.3 253.2 %reduce-scatter.8.cloned.1.call-start = ((), (), s32[]{:S(2)}) async-start(), calls=%async_computation.5 | async-start | bytes 4259840 | tf_op jit(solution)/shard_map/reduce_scatter | solution.py:33
  284.3 402.4 %all-reduce.4.cloned.1.call-start = ((), (), s32[]{:S(2)}) async-start(), calls=%async_computation.6 | async-start | bytes 2097152 | tf_op jit(solution)/shard_map/psum | solution.py:28
  428.5 497.0 %all-gather.7.cloned.1.call-start = ((), (), s32[]{:S(2)}) async-start(), calls=%async_computation.7 | async-start | bytes 2129920 | tf_op jit(solution)/shard_map/all_gather | solution.py:68
  689.7 1.0 copy-start.2
  742.8 102.5 %copy-start.3 = (f32[32,512]{1,0:T(8,128)S(1)}, f32[32,512]{1,0:T(8,128)}, u32[]{:S(2)}) copy-start(f32[32,512]{1,0:T(8,128)} %reduce-scatter.8.cloned.1.call-done) | copy-start | bytes 196612
  850.1 102.1 %reduce-scatter.10.cloned.1.call-start = ((), (), s32[]{:S(2)}) async-start(), calls=%async_computation.9 | async-start | bytes 655360
Sparse Core Ops, SparseCore 0:
  18.3 121.2 all-gather.8
  428.6 258.0 all-reduce.3
  929.3 22.8 reduce-scatter.9
Sparse Core Ops, SparseCore 1:
  22.8 147.9 reduce-scatter.5
  174.0 75.7 all-gather.4
  284.4 141.0 reduce-scatter.7
  850.2 75.2 all-gather.6
